TPU v7x, 32 devices: a whole 2x2x4 slice. The times are simulated.
32 devices in a mesh: req: 16 (over z, x, core), head: 2 (over y).
Axes of the slice: x: 2, y: 2, z: 4, core: 2. Of those that a mesh axis runs over, the one named last changes fastest.
Arguments:
- draft_ids: int32 [256, 16], P('req'), may hold values from 0 to 63999
- worker_slot: int32 [256], P('req'), may hold values from 0 to 255, as said below
- accepted: int32 [256], P('req'), may hold values from 0 to 16
- embedding: bfloat16 [64000, 2048], P('req', 'head'), may hold values from -120 to 120
- w_query: bfloat16 [2048, 2048], P('req', 'head'), may hold values from -0.125 to 0.125
- w_key: bfloat16 [2048, 2048], P('req', 'head'), may hold values from -0.125 to 0.125
- w_value: bfloat16 [2048, 4096], P('req', 'head'), may hold values from -0.125 to 0.125
- w_gate: bfloat16 [2048, 4096], P('req', 'head'), may hold values from -0.125 to 0.125
- old_state: bfloat16 [256, 8, 256, 512], P('req', 'head'), may hold values from -4 to 4
Outputs:
- hidden: bfloat16 [256, 16, 4096], P('req', None, 'head')
- new_state: bfloat16 [256, 8, 256, 512], P('req', 'head')
Inputs may be any that keep to these rules, and one draw needn't show every extreme that they name: worker_slot is a permutation of 0 to 255; request r is handled by worker worker_slot[r] // 16 at position worker_slot[r] % 16; the 16 requests of one owner (aligned blocks of 16) go to 16 different workers.
All inputs are finite; a program needn't handle non-finite values.
Results may differ from a plain program's by a relative error of at most 0.0095.
Values may be sent and summed in bfloat16 or wider, within the bound.
No kernel may reach another device: no remote copies, remote signals or barrier semaphores. Data moves between devices by JAX's collectives and lax.ppermute only.
A program may use at most 192 MiB of HBM per device.

v0:
```python
import jax
import jax.numpy as jnp
from jax import lax
from jax.sharding import PartitionSpec as P


def layer_norm(values):
    center = jnp.mean(values, axis=-1, keepdims=True)
    shifted = values - center
    spread = jnp.mean(shifted * shifted, axis=-1, keepdims=True)
    return shifted * lax.rsqrt(spread + 1e-05)


def add_rows(normed, piece):
    return jnp.dot(normed, piece, preferred_element_type=jnp.float32)


def retention(queries, keys_scaled, values_all, gates_all, start_state, counts_int, head_ids):
    row_count = queries.shape[0]
    draft_len = queries.shape[1]
    heads_dev = start_state.shape[1]
    key_dim = start_state.shape[2]
    value_dim = start_state.shape[3]
    query_heads = queries.reshape(row_count, draft_len, heads_dev, key_dim)
    key_heads = keys_scaled.reshape(row_count, draft_len, heads_dev, key_dim)
    value_heads = values_all.reshape(row_count, draft_len, heads_dev, value_dim)
    gate_heads = gates_all.reshape(row_count, draft_len, heads_dev, value_dim)
    decay_rate = 1.0 - jnp.exp2(-5.0 - head_ids)
    positions = jnp.arange(draft_len, dtype=jnp.float32)
    distance = positions[:, None] - positions[None, :]
    causal = distance >= 0.0
    decay_mask = jnp.where(
        causal[None], jnp.power(decay_rate[:, None, None], jnp.maximum(distance, 0.0)[None]), 0.0
    )
    scores = (
        jnp.einsum("nthk,nshk->nhts", query_heads, key_heads, preferred_element_type=jnp.float32)
        * decay_mask[None]
    )
    weights = scores.astype(jnp.bfloat16)
    inside_terms = jnp.einsum(
        "nhts,nshv->nthv", weights, value_heads, preferred_element_type=jnp.float32
    )
    state_terms = jnp.einsum(
        "nthk,nhkv->nthv", query_heads, start_state, preferred_element_type=jnp.float32
    )
    state_terms = (
        state_terms * jnp.power(decay_rate[None, :], positions[:, None] + 1.0)[None, :, :, None]
    )
    mixture = layer_norm(inside_terms + state_terms)
    hidden = (jax.nn.silu(gate_heads.astype(jnp.float32)) * mixture).astype(jnp.bfloat16)
    hidden = hidden.reshape(row_count, draft_len, heads_dev * value_dim)
    counts = counts_int.astype(jnp.float32)[:, None]
    remaining = jnp.maximum(counts - 1.0 - positions[None, :], 0.0)
    within = positions[None, :] < counts
    scale_rows = jnp.where(
        within[:, :, None], jnp.power(decay_rate[None, None, :], remaining[:, :, None]), 0.0
    )
    kept_keys = (key_heads.astype(jnp.float32) * scale_rows[..., None]).astype(jnp.bfloat16)
    updated = jnp.einsum(
        "nshk,nshv->nhkv", kept_keys, value_heads, preferred_element_type=jnp.float32
    )
    updated = updated + jnp.power(decay_rate[None, :], counts)[
        :, :, None, None
    ] * start_state.astype(jnp.float32)
    return (hidden, updated.astype(jnp.bfloat16))


def per_device(
    draft_ids, worker_slot, accepted, embedding, w_query, w_key, w_value, w_gate, old_state
):
    own_rows = worker_slot.shape[0]
    width_req = lax.axis_size("req")
    my_index = lax.axis_index("req")
    all_ids, all_slots, all_counts = (
        lax.all_gather(draft_ids, "req", axis=0, tiled=True),
        lax.all_gather(worker_slot, "req", axis=0, tiled=True),
        lax.all_gather(accepted, "req", axis=0, tiled=True),
    )
    total_rows = all_slots.shape[0]
    holder = (
        jnp.zeros((total_rows,), jnp.int32)
        .at[all_slots]
        .set(jnp.arange(total_rows, dtype=jnp.int32))
    )
    vocab_rows = embedding.shape[0]
    local_ids = all_ids - my_index * vocab_rows
    inside = (local_ids >= 0) & (local_ids < vocab_rows)
    looked = jnp.take(embedding, jnp.clip(local_ids, 0, vocab_rows - 1), axis=0)
    partial_rows = jnp.where(inside[:, :, None], looked.astype(jnp.float32), 0.0)
    token_cols = lax.psum_scatter(
        partial_rows.astype(jnp.bfloat16), "req", scatter_dimension=0, tiled=True
    )
    tokens = lax.all_gather(token_cols, "head", axis=2, tiled=True)
    draft_len = tokens.shape[1]
    normed = (
        layer_norm(tokens.astype(jnp.float32))
        .astype(jnp.bfloat16)
        .reshape(own_rows * draft_len, tokens.shape[2])
    )

    def add_one(piece):
        return add_rows(normed, piece)

    raw_query = add_one(lax.all_gather(w_query, "req", axis=0, tiled=True))
    raw_key = add_one(lax.all_gather(w_key, "req", axis=0, tiled=True))
    raw_value = add_one(lax.all_gather(w_value, "req", axis=0, tiled=True))
    raw_gate = add_one(lax.all_gather(w_gate, "req", axis=0, tiled=True))
    key_scale = old_state.shape[2] ** (-0.5)
    queries = raw_query.astype(jnp.bfloat16).reshape(own_rows, draft_len, -1)
    keys_scaled = (raw_key * key_scale).astype(jnp.bfloat16).reshape(own_rows, draft_len, -1)
    values_all = raw_value.astype(jnp.bfloat16).reshape(own_rows, draft_len, -1)
    gates_all = raw_gate.astype(jnp.bfloat16).reshape(own_rows, draft_len, -1)
    heads_dev = old_state.shape[1]
    head_ids = (lax.axis_index("head") * heads_dev + jnp.arange(heads_dev, dtype=jnp.int32)).astype(
        jnp.float32
    )
    my_requests = lax.dynamic_slice_in_dim(holder, my_index * own_rows, own_rows)
    source = my_requests // own_rows
    target = worker_slot // own_rows
    to_worker = (
        jnp.zeros((width_req,), jnp.int32).at[target].set(jnp.arange(own_rows, dtype=jnp.int32))
    )
    answer, new_state = retention(
        queries, keys_scaled, values_all, gates_all, old_state, accepted, head_ids
    )
    received = lax.all_to_all(
        jnp.take(answer, to_worker, axis=0), "req", split_axis=0, concat_axis=0, tiled=True
    )
    hidden = jnp.take(received, source, axis=0)
    return (hidden, new_state)


def solution(mesh):
    return jax.shard_map(
        per_device,
        mesh=mesh,
        in_specs=(
            P("req", None),
            P("req"),
            P("req"),
            P("req", "head"),
            P("req", "head"),
            P("req", "head"),
            P("req", "head"),
            P("req", "head"),
            P("req", "head", None, None),
        ),
        out_specs=(P("req", None, "head"), P("req", "head", None, None)),
        check_vma=False,
    )
```

profile of v0, /device:TPU:11, one launch (start us, length us, event | category | flops | bytes accessed | tf_op | source)
XLA Modules:
  0.0 497.8 jit_solution(5932785029727653407)
XLA Ops:
  7.2 16.2 %all_gather.21 = s32[256,16]{1,0:T(8,128)S(1)} all-gather(s32[16,16]{1,0:T(8,128)} %param.11), channel_id=1, replica_groups=mesh['req'=16,'head'=2] {'req'}, dimensions={0}, use_global_device_ids=true | all-gather | bytes 17408 | tf_op jit(solution)/shard_map/all_gather | solution.py:75
  24.0 25.2 %gather_fusion = bf16[4096,1024]{1,0:T(8,128)(2,1)} fusion(bf16[4000,1024]{1,0:T(8,128)(2,1)} %param.14, s32[4096]{0:T(1024)S(1)} %broadcast_clamp_fusion), kind=kCustom, calls=%fused_computation.2 | custom fusion | bytes 16793600 | tf_op jit(solution)/shard_map/jit(_take)/gather | solution.py:88
  49.2 7.9 %select_convert_fusion = bf16[256,16,1024]{2,1,0:T(8,128)(2,1)} fusion(bf16[256,16,1024]{2,1,0:T(8,128)(2,1)} %bitcast.21, pred[256,16]{1,0:T(8,128)(4,1)S(1)} %copy.42, pred[256,16]{1,0:T(8,128)(4,1)S(1)} %copy.41), kind=kLoop, calls=%fused_computation.6 | loop fusion | flops 16777216 | bytes 16785408 | tf_op jit(solution)/shard_map/convert_element_type | solution.py:91
  57.2 107.9 %reduce-scatter.2.cloned.1.call-done = bf16[16,16,1024]{2,1,0:T(8,128)(2,1)} async-done(((bf16[256,16,1024]{2,1,0:T(8,128)(2,1)}), bf16[16,16,1024]{2,1,0:T(8,128)(2,1)}) %reduce-scatter.2.cloned.1.call-update) | async-done | bytes 524304 | tf_op jit(solution)/shard_map/reduce_scatter | solution.py:90
  170.0 7.4 %all-reduce = s32[256]{0:T(256)S(1)} all-reduce(s32[256]{0:T(256)S(1)} %dynamic-update-slice), channel_id=1, replica_groups=mesh['req'=16,'head'=2] {'req'}, use_global_device_ids=true, to_apply=%add | all-reduce | flops 256 | bytes 2048
  179.2 8.5 %all-gather.6.cloned.1.call-done = bf16[16,16,2048]{2,1,0:T(8,128)(2,1)} async-done(((bf16[16,16,1024]{2,1,0:T(8,128)(2,1)}), bf16[16,16,2048]{2,1,0:T(8,128)(2,1)}) %all-gather.6.cloned.1.call-update) | async-done | bytes 1048592 | tf_op jit(solution)/shard_map/all_gather | solution.py:93
  189.2 1.6 fusion.3
  192.4 47.8 %all-gather.12.cloned.1.call-done = bf16[2048,1024]{1,0:T(8,128)(2,1)} async-done(((bf16[128,1024]{1,0:T(8,128)(2,1)}), bf16[2048,1024]{1,0:T(8,128)(2,1)}) %all-gather.12.cloned.1.call-update) | async-done | bytes 4194320 | tf_op jit(solution)/shard_map/all_gather | solution.py:104
  240.2 3.4 convolution_convert_fusion.2
  244.0 47.3 %all-gather.14.cloned.1.call-done = bf16[2048,1024]{1,0:T(8,128)(2,1)} async-done(((bf16[128,1024]{1,0:T(8,128)(2,1)}), bf16[2048,1024]{1,0:T(8,128)(2,1)}) %all-gather.14.cloned.1.call-update) | async-done | bytes 4194320 | tf_op jit(solution)/shard_map/all_gather | solution.py:105
  291.3 3.4 fusion.6
  295.9 9.8 %fusion.15 = f32[16,4,16,512]{3,2,1,0:T(8,128)} fusion(bf16[16,4,256,512]{3,2,1,0:T(8,128)(2,1)} %param.19, bf16[16,16,4,256]{3,2,1,0:T(4,128)(2,1)S(1)} %reshape_reshape.11), kind=kOutput, calls=%fused_computation.34 | convolution fusion | flops 268435456 | bytes 19398656 | tf_op jit(solution)/shard_map/nthk,nhkv->nthv/dot_general | solution.py:43
  305.7 60.4 %all-gather.10.cloned.1.call-done = bf16[2048,2048]{1,0:T(8,128)(2,1)} async-done(((bf16[128,2048]{1,0:T(8,128)(2,1)}), bf16[2048,2048]{1,0:T(8,128)(2,1)}) %all-gather.10.cloned.1.call-update) | async-done | bytes 8388624 | tf_op jit(solution)/shard_map/all_gather | solution.py:106
  366.1 6.7 %convolution_convert_fusion = bf16[256,2048]{1,0:T(8,128)(2,1)} fusion(bf16[256,2048]{1,0:T(8,128)(2,1)S(1)} %bitcast.25, bf16[2048,2048]{1,0:T(8,128)(2,1)} %all-gather.10.cloned.1.call-done), kind=kOutput, calls=%fused_computation.9 | convolution fusion | flops 2148007936 | bytes 10485760 | tf_op jit(solution)/shard_map/dot_general | solution.py:15
  372.8 1.8 reshape_reshape.10
  374.6 2.9 fusion.26
  378.1 63.2 %all-gather.8.cloned.1.call-done = bf16[2048,2048]{1,0:T(8,128)(2,1)} async-done(((bf16[128,2048]{1,0:T(8,128)(2,1)}), bf16[2048,2048]{1,0:T(8,128)(2,1)}) %all-gather.8.cloned.1.call-update) | async-done | bytes 8388624 | tf_op jit(solution)/shard_map/all_gather | solution.py:107
  441.3 7.4 %fusion = f32[256,2048]{1,0:T(8,128)} fusion(bf16[256,2048]{1,0:T(8,128)(2,1)} %bitcast.26, bf16[2048,2048]{1,0:T(8,128)(2,1)} %all-gather.8.cloned.1.call-done), kind=kOutput, calls=%fused_computation.11 | convolution fusion | flops 2148532224 | bytes 11534336 | tf_op jit(solution)/shard_map/dot_general | solution.py:15
  448.7 3.7 reshape.209
  452.3 2.5 fusion.8
  455.9 1.8 gather_fusion.1
  458.9 5.4 %all-to-all-start = ((bf16[16,16,2048]{2,1,0:T(8,128)(2,1)}), bf16[16,16,2048]{2,1,0:T(8,128)(2,1)S(1)}, u32[]{:S(2)}, u32[]{:S(2)}) async-start(bf16[16,16,2048]{2,1,0:T(8,128)(2,1)} %broadcast_select_fusion.1), calls=%async_computation.1 | async-start | bytes 2097152 | tf_op jit(solution)/shard_map/all_to_all | solution.py:126
  464.6 19.5 %add_convert_fusion = bf16[16,4,256,512]{3,2,1,0:T(8,128)(2,1)} fusion(bf16[16,4,256,512]{3,2,1,0:T(8,128)(2,1)} %param.19, f32[16,4]{1,0:T(8,128)S(1)} %copy.53, bf16[16,16,4,512]{3,2,1,0:T(4,128)(2,1)S(1)} %reshape_reshape.10, f32[16,16,4]{1,2,0:T(4,128)S(1)} %power_select_fusion, bf16[16,16,4,256]{3,2,1,0:T(4,128)(2,1)S(1)} %copy-done.1), kind=kOutput, calls=%fused_computation.5 | convolution fusion | flops 302776320 | bytes 35131648 | tf_op jit(solution)/shard_map/nshk,nshv->nhkv/dot_general | solution.py:59
  484.1 5.2 %all-to-all-done = bf16[16,16,2048]{2,1,0:T(8,128)(2,1)S(1)} async-done(((bf16[16,16,2048]{2,1,0:T(8,128)(2,1)}), bf16[16,16,2048]{2,1,0:T(8,128)(2,1)S(1)}, u32[]{:S(2)}, u32[]{:S(2)}) %all-to-all-start) | async-done | bytes 1048608 | tf_op jit(solution)/shard_map/all_to_all | solution.py:126
  (70 shorter events, 15.8 us)
Async XLA Ops:
  7.2 158.0 %reduce-scatter.2.cloned.1.call-start = ((), (), s32[]{:S(2)}) async-start(), calls=%async_computation.2 | async-start | bytes 8912896 | tf_op jit(solution)/shard_map/reduce_scatter | solution.py:90
  57.1 110.5 %copy-start.4 = (s32[16]{0:T(128)S(1)}, s32[16]{0:T(128)}, u32[]{:S(2)}) copy-start(s32[16]{0:T(128)} %param.13) | copy-start | bytes 196
  57.1 110.8 %copy-start.3 = (s32[16]{0:T(128)S(1)}, s32[16]{0:T(128)}, u32[]{:S(2)}) copy-start(s32[16]{0:T(128)} %param.12) | copy-start | bytes 196
  57.1 111.4 %copy-start.5 = (u32[32]{0:T(128)S(1)}, u32[32]{0:T(128)}, u32[]{:S(2)}) copy-start(u32[32]{0:T(128)} %constant.98) | copy-start | bytes 388
  57.1 130.6 %all-gather.6.cloned.1.call-start = ((), (), s32[]{:S(2)}) async-start(), calls=%async_computation.3 | async-start | bytes 1572864 | tf_op jit(solution)/shard_map/all_gather | solution.py:93
  165.2 75.0 %all-gather.12.cloned.1.call-start = ((), (), s32[]{:S(2)}) async-start(), calls=%async_computation.6 | async-start | bytes 4456448 | tf_op jit(solution)/shard_map/all_gather | solution.py:104
  165.9 125.4 %all-gather.14.cloned.1.call-start = ((), (), s32[]{:S(2)}) async-start(), calls=%async_computation.7 | async-start | bytes 4456448 | tf_op jit(solution)/shard_map/all_gather | solution.py:105
  166.5 199.6 %all-gather.10.cloned.1.call-start = ((), (), s32[]{:S(2)}) async-start(), calls=%async_computation.5 | async-start | bytes 8912896 | tf_op jit(solution)/shard_map/all_gather | solution.py:106
  167.0 274.2 %all-gather.8.cloned.1.call-start = ((), (), s32[]{:S(2)}) async-start(), calls=%async_computation.4 | async-start | bytes 8912896 | tf_op jit(solution)/shard_map/all_gather | solution.py:107
  192.4 173.7 %copy-start.2 = (bf16[16,16,2048]{2,1,0:T(8,128)(2,1)}, bf16[16,16,2048]{2,1,0:T(8,128)(2,1)S(1)}, u32[]{:S(2)}) copy-start(bf16[16,16,2048]{2,1,0:T(8,128)(2,1)S(1)} %fusion.4) | copy-start | bytes 3145732
  244.0 51.9 %copy-start = (bf16[16,16,4,256]{3,2,1,0:T(4,128)(2,1)}, bf16[16,16,4,256]{3,2,1,0:T(4,128)(2,1)S(1)}, u32[]{:S(2)}) copy-start(bf16[16,16,4,256]{3,2,1,0:T(4,128)(2,1)S(1)} %reshape_reshape.11) | copy-start | bytes 1572868
  454.8 9.7 %copy-start.1 = (bf16[16,16,4,256]{3,2,1,0:T(4,128)(2,1)S(1)}, bf16[16,16,4,256]{3,2,1,0:T(4,128)(2,1)}, u32[]{:S(2)}) copy-start(bf16[16,16,4,256]{3,2,1,0:T(4,128)(2,1)} %reshape_reshape.12) | copy-start | bytes 1572868
  458.9 30.3 %all-to-all-start = ((bf16[16,16,2048]{2,1,0:T(8,128)(2,1)}), bf16[16,16,2048]{2,1,0:T(8,128)(2,1)S(1)}, u32[]{:S(2)}, u32[]{:S(2)}) async-start(bf16[16,16,2048]{2,1,0:T(8,128)(2,1)} %broadcast_select_fusion.1), calls=%async_computation.1 | async-start | bytes 2097152 | tf_op jit(solution)/shard_map/all_to_all | solution.py:126
Sparse Core Ops, SparseCore 0:
  57.3 107.8 reduce-scatter.1
  166.7 21.0 all-gather.5
  189.9 50.2 all-gather.11
  242.2 49.0 all-gather.13
  293.3 72.7 all-gather.9
  368.1 73.1 all-gather.7
where the time goes:
time: 499 us; the launch traced here: 498 us
  waiting for transfers between devices  343 us (69%)
  matrix products  53 us (11%)
  local copies, waits for them, and re-layouts  39.3 us (8%)
  blocking collectives  23.6 us (5%)
  other arithmetic  18.4 us (4%)
  between operations  15.1 us (3%)
  starting transfers between devices  5.64 us (1%)
    reduce_scatter x1, waiting for transfers between devices, per_device(): lax.psum_scatter(partial_rows.astype(jnp.bfloat16), 'req', scatter_dimens...  108 us
    all_gather x1, waiting for transfers between devices, per_device(): raw_gate = add_one(lax.all_gather(w_gate, 'req', axis=0, tiled=True))  63.2 us
    all_gather x1, waiting for transfers between devices, per_device(): raw_value = add_one(lax.all_gather(w_value, 'req', axis=0, tiled=True))  60.4 us
    all_gather x1, waiting for transfers between devices, per_device(): raw_query = add_one(lax.all_gather(w_query, 'req', axis=0, tiled=True))  47.8 us
    all_gather x1, waiting for transfers between devices, per_device(): raw_key = add_one(lax.all_gather(w_key, 'req', axis=0, tiled=True))  47.3 us
    gather x1, local copies, waits for them, and re-layouts, per_device(): looked = jnp.take(embedding, jnp.clip(local_ids, 0, vocab_rows - 1), axis=0)  25.2 us
    dot_general x4, matrix products, add_rows(): return jnp.dot(normed, piece, preferred_element_type=jnp.float32)  20.9 us
    dot_general x1, matrix products, retention(): jnp.einsum('nshk,nshv->nhkv', kept_keys, value_heads, preferred_element_t...  19.5 us
  transfers between devices with their start and end apart: 7, of which 7 were waited for; matrix products, arithmetic and copies ran while one was open for 12% of the time, Pallas kernels for 0%

commit v1 on v0

--- a/solution.py
+++ b/solution.py
@@ -123,9 +123,20 @@
     answer, new_state = retention(
         queries, keys_scaled, values_all, gates_all, old_state, accepted, head_ids
     )
-    received = lax.all_to_all(
-        jnp.take(answer, to_worker, axis=0), "req", split_axis=0, concat_axis=0, tiled=True
-    )
+    array = jnp.take(answer, to_worker, axis=0)
+    ways, here = (lax.axis_size("req"), lax.axis_index("req"))
+    width = array.shape[0] // ways
+    lengths = list(array.shape)
+    lengths[0] = width
+    height = lengths[0]
+    lengths[0] = height * ways
+    full = jnp.zeros(lengths, array.dtype)
+    for mask in range(ways):
+        part = lax.dynamic_slice_in_dim(array, (here ^ mask) * width, width, axis=0)
+        if mask:
+            part = lax.ppermute(part, "req", [(d, d ^ mask) for d in range(ways)])
+        full = lax.dynamic_update_slice_in_dim(full, part, (here ^ mask) * height, axis=0)
+    received = full
     hidden = jnp.take(received, source, axis=0)
     return (hidden, new_state)
 

time: 499 us -> 523 us (1.048)
  starting transfers between devices: 5.64 us -> 18.1 us
  waiting for transfers between devices: 343 us -> 349 us
  local copies, waits for them, and re-layouts: 39.3 us -> 44.7 us
    ppermute x0 -> x15, starting transfers between devices: none -> 17.9 us  [per_device(): part = lax.ppermute(part, 'req', [(d, d ^ mask) for d in range(ways)])]
    ppermute x0 -> x15, waiting for transfers between devices: none -> 12.5 us  [per_device(): part = lax.ppermute(part, 'req', [(d, d ^ mask) for d in range(ways)])]
    all_to_all x1 -> x0, starting transfers between devices: 5.41 us -> none  [per_device(): lax.all_to_all(jnp.take(answer, to_worker, axis=0), 'req', split_axis=0,...]
  transfers between devices with their start and end apart: 7 -> 21, of which waited for: 7 -> 10; matrix products, arithmetic and copies ran while one was open for 12% -> 12% of each run, Pallas kernels for 0% -> 0%
where the time goes in v1:
time: 523 us; the launch traced here: 522 us
  waiting for transfers between devices  349 us (67%)
  matrix products  53 us (10%)
  local copies, waits for them, and re-layouts  44.7 us (9%)
  blocking collectives  23.6 us (5%)
  starting transfers between devices  18.1 us (3%)
  other arithmetic  17.5 us (3%)
  between operations  15.3 us (3%)
    reduce_scatter x1, waiting for transfers between devices, per_device(): lax.psum_scatter(partial_rows.astype(jnp.bfloat16), 'req', scatter_dimens...  108 us
    all_gather x1, waiting for transfers between devices, per_device(): raw_gate = add_one(lax.all_gather(w_gate, 'req', axis=0, tiled=True))  63.2 us
    all_gather x1, waiting for transfers between devices, per_device(): raw_value = add_one(lax.all_gather(w_value, 'req', axis=0, tiled=True))  60.4 us
    all_gather x1, waiting for transfers between devices, per_device(): raw_query = add_one(lax.all_gather(w_query, 'req', axis=0, tiled=True))  47.8 us
    all_gather x1, waiting for transfers between devices, per_device(): raw_key = add_one(lax.all_gather(w_key, 'req', axis=0, tiled=True))  47.3 us
    gather x1, local copies, waits for them, and re-layouts, per_device(): looked = jnp.take(embedding, jnp.clip(local_ids, 0, vocab_rows - 1), axis=0)  25.2 us
    dot_general x4, matrix products, add_rows(): return jnp.dot(normed, piece, preferred_element_type=jnp.float32)  20.9 us
    dot_general x1, matrix products, retention(): jnp.einsum('nshk,nshv->nhkv', kept_keys, value_heads, preferred_element_t...  19.5 us
  transfers between devices with their start and end apart: 21, of which 10 were waited for; matrix products, arithmetic and copies ran while one was open for 12% of the time, Pallas kernels for 0%

profile of v1, /device:TPU:11, one launch (start us, length us, event | category | flops | bytes accessed | tf_op | source)
XLA Modules:
  0.0 521.7 jit_solution(17641157134163181821)
XLA Ops:
  7.2 16.2 %all_gather.21 = s32[256,16]{1,0:T(8,128)S(1)} all-gather(s32[16,16]{1,0:T(8,128)} %param.11), channel_id=1, replica_groups=mesh['req'=16,'head'=2] {'req'}, dimensions={0}, use_global_device_ids=true | all-gather | bytes 17408 | tf_op jit(solution)/shard_map/all_gather | solution.py:75
  24.0 25.2 %gather_fusion = bf16[4096,1024]{1,0:T(8,128)(2,1)} fusion(bf16[4000,1024]{1,0:T(8,128)(2,1)} %param.14, s32[4096]{0:T(1024)S(1)} %broadcast_clamp_fusion), kind=kCustom, calls=%fused_computation.2 | custom fusion | bytes 16793600 | tf_op jit(solution)/shard_map/jit(_take)/gather | solution.py:88
  49.2 7.9 %select_convert_fusion = bf16[256,16,1024]{2,1,0:T(8,128)(2,1)} fusion(bf16[256,16,1024]{2,1,0:T(8,128)(2,1)} %bitcast.21, pred[256,16]{1,0:T(8,128)(4,1)S(1)} %copy.42, pred[256,16]{1,0:T(8,128)(4,1)S(1)} %copy.41), kind=kLoop, calls=%fused_computation.6 | loop fusion | flops 16777216 | bytes 16785408 | tf_op jit(solution)/shard_map/convert_element_type | solution.py:91
  57.2 107.9 %reduce-scatter.2.cloned.1.call-done = bf16[16,16,1024]{2,1,0:T(8,128)(2,1)} async-done(((bf16[256,16,1024]{2,1,0:T(8,128)(2,1)}), bf16[16,16,1024]{2,1,0:T(8,128)(2,1)}) %reduce-scatter.2.cloned.1.call-update) | async-done | bytes 524304 | tf_op jit(solution)/shard_map/reduce_scatter | solution.py:90
  170.2 7.4 %all-reduce = s32[256]{0:T(256)S(1)} all-reduce(s32[256]{0:T(256)S(1)} %dynamic-update-slice), channel_id=1, replica_groups=mesh['req'=16,'head'=2] {'req'}, use_global_device_ids=true, to_apply=%add | all-reduce | flops 256 | bytes 2048
  179.8 7.9 %all-gather.6.cloned.1.call-done = bf16[16,16,2048]{2,1,0:T(8,128)(2,1)} async-done(((bf16[16,16,1024]{2,1,0:T(8,128)(2,1)}), bf16[16,16,2048]{2,1,0:T(8,128)(2,1)}) %all-gather.6.cloned.1.call-update) | async-done | bytes 1048592 | tf_op jit(solution)/shard_map/all_gather | solution.py:93
  192.4 47.8 %all-gather.12.cloned.1.call-done = bf16[2048,1024]{1,0:T(8,128)(2,1)} async-done(((bf16[128,1024]{1,0:T(8,128)(2,1)}), bf16[2048,1024]{1,0:T(8,128)(2,1)}) %all-gather.12.cloned.1.call-update) | async-done | bytes 4194320 | tf_op jit(solution)/shard_map/all_gather | solution.py:104
  240.2 3.4 convolution_convert_fusion.2
  244.0 47.3 %all-gather.14.cloned.1.call-done = bf16[2048,1024]{1,0:T(8,128)(2,1)} async-done(((bf16[128,1024]{1,0:T(8,128)(2,1)}), bf16[2048,1024]{1,0:T(8,128)(2,1)}) %all-gather.14.cloned.1.call-update) | async-done | bytes 4194320 | tf_op jit(solution)/shard_map/all_gather | solution.py:105
  291.3 3.4 fusion.6
  295.9 9.8 %fusion.15 = f32[16,4,16,512]{3,2,1,0:T(8,128)} fusion(bf16[16,4,256,512]{3,2,1,0:T(8,128)(2,1)} %param.19, bf16[16,16,4,256]{3,2,1,0:T(4,128)(2,1)S(1)} %reshape_reshape.11), kind=kOutput, calls=%fused_computation.34 | convolution fusion | flops 268435456 | bytes 19398656 | tf_op jit(solution)/shard_map/nthk,nhkv->nthv/dot_general | solution.py:43
  305.7 60.4 %all-gather.10.cloned.1.call-done = bf16[2048,2048]{1,0:T(8,128)(2,1)} async-done(((bf16[128,2048]{1,0:T(8,128)(2,1)}), bf16[2048,2048]{1,0:T(8,128)(2,1)}) %all-gather.10.cloned.1.call-update) | async-done | bytes 8388624 | tf_op jit(solution)/shard_map/all_gather | solution.py:106
  366.1 6.7 %convolution_convert_fusion = bf16[256,2048]{1,0:T(8,128)(2,1)} fusion(bf16[256,2048]{1,0:T(8,128)(2,1)S(1)} %bitcast.25, bf16[2048,2048]{1,0:T(8,128)(2,1)} %all-gather.10.cloned.1.call-done), kind=kOutput, calls=%fused_computation.9 | convolution fusion | flops 2148007936 | bytes 10485760 | tf_op jit(solution)/shard_map/dot_general | solution.py:15
  374.6 2.9 fusion.26
  378.1 63.2 %all-gather.8.cloned.1.call-done = bf16[2048,2048]{1,0:T(8,128)(2,1)} async-done(((bf16[128,2048]{1,0:T(8,128)(2,1)}), bf16[2048,2048]{1,0:T(8,128)(2,1)}) %all-gather.8.cloned.1.call-update) | async-done | bytes 8388624 | tf_op jit(solution)/shard_map/all_gather | solution.py:107
  441.3 7.4 %fusion = f32[256,2048]{1,0:T(8,128)} fusion(bf16[256,2048]{1,0:T(8,128)(2,1)} %bitcast.26, bf16[2048,2048]{1,0:T(8,128)(2,1)} %all-gather.8.cloned.1.call-done), kind=kOutput, calls=%fused_computation.11 | convolution fusion | flops 2148532224 | bytes 11534336 | tf_op jit(solution)/shard_map/dot_general | solution.py:15
  448.7 3.6 reshape.209
  452.3 2.5 fusion.8
  462.6 19.5 %add_convert_fusion = bf16[16,4,256,512]{3,2,1,0:T(8,128)(2,1)} fusion(bf16[16,4,256,512]{3,2,1,0:T(8,128)(2,1)} %param.19, f32[16,4]{1,0:T(8,128)S(1)} %copy.53, bf16[16,16,4,512]{3,2,1,0:T(4,128)(2,1)S(1)} %reshape_reshape.10, f32[16,16,4]{1,2,0:T(4,128)S(1)} %power_select_fusion, bf16[16,16,4,256]{3,2,1,0:T(4,128)(2,1)S(1)} %copy-done.1), kind=kOutput, calls=%fused_computation.5 | convolution fusion | flops 302776320 | bytes 35131648 | tf_op jit(solution)/shard_map/nshk,nshv->nhkv/dot_general | solution.py:59
  490.9 1.9 collective-permute-start.9
  497.4 1.9 collective-permute-start.13
  500.6 6.6 %collective-permute-done.11 = bf16[1,16,2048]{2,1,0:T(8,128)(2,1)S(1)} collective-permute-done((bf16[1,16,2048]{2,1,0:T(8,128)(2,1)S(1)}, bf16[1,16,2048]{2,1,0:T(8,128)(2,1)S(1)}, u32[]{:S(2)}, u32[]{:S(2)}) %collective-permute-start.11) | collective-permute-done | bytes 65568 | tf_op jit(solution)/shard_map/ppermute | solution.py:137
  507.2 2.5 collective-permute-done.12
  509.7 1.9 collective-permute-done.13
  (115 shorter events, 41.0 us)
Async XLA Ops:
  7.2 158.0 %reduce-scatter.2.cloned.1.call-start = ((), (), s32[]{:S(2)}) async-start(), calls=%async_computation.1 | async-start | bytes 8912896 | tf_op jit(solution)/shard_map/reduce_scatter | solution.py:90
  57.1 110.8 %copy-start.3 = (s32[16]{0:T(128)S(1)}, s32[16]{0:T(128)}, u32[]{:S(2)}) copy-start(s32[16]{0:T(128)} %param.12) | copy-start | bytes 196
  57.1 111.6 %copy-start.5 = (u32[32]{0:T(128)S(1)}, u32[32]{0:T(128)}, u32[]{:S(2)}) copy-start(u32[32]{0:T(128)} %constant.126) | copy-start | bytes 388
  57.1 130.6 %all-gather.6.cloned.1.call-start = ((), (), s32[]{:S(2)}) async-start(), calls=%async_computation.2 | async-start | bytes 1572864 | tf_op jit(solution)/shard_map/all_gather | solution.py:93
  165.2 75.0 %all-gather.12.cloned.1.call-start = ((), (), s32[]{:S(2)}) async-start(), calls=%async_computation.5 | async-start | bytes 4456448 | tf_op jit(solution)/shard_map/all_gather | solution.py:104
  165.9 125.4 %all-gather.14.cloned.1.call-start = ((), (), s32[]{:S(2)}) async-start(), calls=%async_computation.6 | async-start | bytes 4456448 | tf_op jit(solution)/shard_map/all_gather | solution.py:105
  166.5 199.6 %all-gather.10.cloned.1.call-start = ((), (), s32[]{:S(2)}) async-start(), calls=%async_computation.4 | async-start | bytes 8912896 | tf_op jit(solution)/shard_map/all_gather | solution.py:106
  167.1 274.2 %all-gather.8.cloned.1.call-start = ((), (), s32[]{:S(2)}) async-start(), calls=%async_computation.3 | async-start | bytes 8912896 | tf_op jit(solution)/shard_map/all_gather | solution.py:107
  192.4 173.7 %copy-start.2 = (bf16[16,16,2048]{2,1,0:T(8,128)(2,1)}, bf16[16,16,2048]{2,1,0:T(8,128)(2,1)S(1)}, u32[]{:S(2)}) copy-start(bf16[16,16,2048]{2,1,0:T(8,128)(2,1)S(1)} %fusion.4) | copy-start | bytes 3145732
  458.9 23.2 %collective-permute-start = (bf16[1,16,2048]{2,1,0:T(8,128)(2,1)}, bf16[1,16,2048]{2,1,0:T(8,128)(2,1)}, u32[]{:S(2)}, u32[]{:S(2)}) collective-permute-start(bf16[1,16,2048]{2,1,0:T(8,128)(2,1)} %get-tuple-element.21), channel_id=1, source_target_pairs={{0,2},{2,0},{4,6},{6,4},{8,10},{10,8},{12,14},{14,12},{16,18},{18,... | collective-permute-start | bytes 196616 | tf_op jit(solution)/shard_map/ppermute | solution.py:137
  459.1 25.6 %collective-permute-start.1 = (bf16[1,16,2048]{2,1,0:T(8,128)(2,1)}, bf16[1,16,2048]{2,1,0:T(8,128)(2,1)}, u32[]{:S(2)}, u32[]{:S(2)}) collective-permute-start(bf16[1,16,2048]{2,1,0:T(8,128)(2,1)} %get-tuple-element.20), channel_id=1, source_target_pairs={{0,4},{2,6},{4,0},{6,2},{8,12},{10,14},{12,8},{14,10},{16,20},{18,... | collective-permute-start | bytes 196616 | tf_op jit(solution)/shard_map/ppermute | solution.py:137
  460.3 26.3 %collective-permute-start.2 = (bf16[1,16,2048]{2,1,0:T(8,128)(2,1)S(1)}, bf16[1,16,2048]{2,1,0:T(8,128)(2,1)}, u32[]{:S(2)}, u32[]{:S(2)}) collective-permute-start(bf16[1,16,2048]{2,1,0:T(8,128)(2,1)S(1)} %get-tuple-element.19), channel_id=1, source_target_pairs={{0,6},{2,4},{4,2},{6,0},{8,14},{10,12},{12,10},{14,8},{16,22},{18,... | collective-permute-start | bytes 196616 | tf_op jit(solution)/shard_map/ppermute | solution.py:137
  461.0 27.6 %collective-permute-start.3 = (bf16[1,16,2048]{2,1,0:T(8,128)(2,1)S(1)}, bf16[1,16,2048]{2,1,0:T(8,128)(2,1)}, u32[]{:S(2)}, u32[]{:S(2)}) collective-permute-start(bf16[1,16,2048]{2,1,0:T(8,128)(2,1)S(1)} %get-tuple-element.18), channel_id=1, source_target_pairs={{0,8},{2,10},{4,12},{6,14},{8,0},{10,2},{12,4},{14,6},{16,24},{18,... | collective-permute-start | bytes 196616 | tf_op jit(solution)/shard_map/ppermute | solution.py:137
  461.9 29.1 %collective-permute-start.4 = (bf16[1,16,2048]{2,1,0:T(8,128)(2,1)S(1)}, bf16[1,16,2048]{2,1,0:T(8,128)(2,1)}, u32[]{:S(2)}, u32[]{:S(2)}) collective-permute-start(bf16[1,16,2048]{2,1,0:T(8,128)(2,1)S(1)} %get-tuple-element.17), channel_id=1, source_target_pairs={{0,10},{2,8},{4,14},{6,12},{8,2},{10,0},{12,6},{14,4},{16,26},{18,... | collective-permute-start | bytes 196616 | tf_op jit(solution)/shard_map/ppermute | solution.py:137
  482.1 11.6 %collective-permute-start.5 = (bf16[1,16,2048]{2,1,0:T(8,128)(2,1)S(1)}, bf16[1,16,2048]{2,1,0:T(8,128)(2,1)S(1)}, u32[]{:S(2)}, u32[]{:S(2)}) collective-permute-start(bf16[1,16,2048]{2,1,0:T(8,128)(2,1)S(1)} %get-tuple-element.16), channel_id=1, source_target_pairs={{0,12},{2,14},{4,8},{6,10},{8,4},{10,6},{12,0},{14,2},{16,28},{18,... | collective-permute-start | bytes 196616 | tf_op jit(solution)/shard_map/ppermute | solution.py:137
  484.7 10.9 %collective-permute-start.6 = (bf16[1,16,2048]{2,1,0:T(8,128)(2,1)S(1)}, bf16[1,16,2048]{2,1,0:T(8,128)(2,1)S(1)}, u32[]{:S(2)}, u32[]{:S(2)}) collective-permute-start(bf16[1,16,2048]{2,1,0:T(8,128)(2,1)S(1)} %get-tuple-element.15), channel_id=1, source_target_pairs={{0,14},{2,12},{4,10},{6,8},{8,6},{10,4},{12,2},{14,0},{16,30},{18,... | collective-permute-start | bytes 196616 | tf_op jit(solution)/shard_map/ppermute | solution.py:137
  486.6 10.1 %collective-permute-start.7 = (bf16[1,16,2048]{2,1,0:T(8,128)(2,1)S(1)}, bf16[1,16,2048]{2,1,0:T(8,128)(2,1)S(1)}, u32[]{:S(2)}, u32[]{:S(2)}) collective-permute-start(bf16[1,16,2048]{2,1,0:T(8,128)(2,1)S(1)} %get-tuple-element.14), channel_id=1, source_target_pairs={{0,16},{2,18},{4,20},{6,22},{8,24},{10,26},{12,28},{14,30},{16,0},... | collective-permute-start | bytes 196616 | tf_op jit(solution)/shard_map/ppermute | solution.py:137
  488.6 8.8 %collective-permute-start.8 = (bf16[1,16,2048]{2,1,0:T(8,128)(2,1)S(1)}, bf16[1,16,2048]{2,1,0:T(8,128)(2,1)S(1)}, u32[]{:S(2)}, u32[]{:S(2)}) collective-permute-start(bf16[1,16,2048]{2,1,0:T(8,128)(2,1)S(1)} %get-tuple-element.13), channel_id=1, source_target_pairs={{0,18},{2,16},{4,22},{6,20},{8,26},{10,24},{12,30},{14,28},{16,2},... | collective-permute-start | bytes 196616 | tf_op jit(solution)/shard_map/ppermute | solution.py:137
  490.9 8.4 %collective-permute-start.9 = (bf16[1,16,2048]{2,1,0:T(8,128)(2,1)S(1)}, bf16[1,16,2048]{2,1,0:T(8,128)(2,1)S(1)}, u32[]{:S(2)}, u32[]{:S(2)}) collective-permute-start(bf16[1,16,2048]{2,1,0:T(8,128)(2,1)S(1)} %get-tuple-element.12), channel_id=1, source_target_pairs={{0,20},{2,22},{4,16},{6,18},{8,28},{10,30},{12,24},{14,26},{16,4},... | collective-permute-start | bytes 196616 | tf_op jit(solution)/shard_map/ppermute | solution.py:137
  493.7 6.8 %collective-permute-start.10 = (bf16[1,16,2048]{2,1,0:T(8,128)(2,1)S(1)}, bf16[1,16,2048]{2,1,0:T(8,128)(2,1)S(1)}, u32[]{:S(2)}, u32[]{:S(2)}) collective-permute-start(bf16[1,16,2048]{2,1,0:T(8,128)(2,1)S(1)} %get-tuple-element.11), channel_id=1, source_target_pairs={{0,22},{2,20},{4,18},{6,16},{8,30},{10,28},{12,26},{14,24},{16,6},... | collective-permute-start | bytes 196616 | tf_op jit(solution)/shard_map/ppermute | solution.py:137
  495.6 11.6 %collective-permute-start.11 = (bf16[1,16,2048]{2,1,0:T(8,128)(2,1)S(1)}, bf16[1,16,2048]{2,1,0:T(8,128)(2,1)S(1)}, u32[]{:S(2)}, u32[]{:S(2)}) collective-permute-start(bf16[1,16,2048]{2,1,0:T(8,128)(2,1)S(1)} %get-tuple-element.10), channel_id=1, source_target_pairs={{0,24},{2,26},{4,28},{6,30},{8,16},{10,18},{12,20},{14,22},{16,8},... | collective-permute-start | bytes 196616 | tf_op jit(solution)/shard_map/ppermute | solution.py:137
  496.7 13.0 %collective-permute-start.12 = (bf16[1,16,2048]{2,1,0:T(8,128)(2,1)S(1)}, bf16[1,16,2048]{2,1,0:T(8,128)(2,1)S(1)}, u32[]{:S(2)}, u32[]{:S(2)}) collective-permute-start(bf16[1,16,2048]{2,1,0:T(8,128)(2,1)S(1)} %get-tuple-element.9), channel_id=1, source_target_pairs={{0,26},{2,24},{4,30},{6,28},{8,18},{10,16},{12,22},{14,20},{16,10}... | collective-permute-start | bytes 196616 | tf_op jit(solution)/shard_map/ppermute | solution.py:137
  497.4 14.2 %collective-permute-start.13 = (bf16[1,16,2048]{2,1,0:T(8,128)(2,1)S(1)}, bf16[1,16,2048]{2,1,0:T(8,128)(2,1)S(1)}, u32[]{:S(2)}, u32[]{:S(2)}) collective-permute-start(bf16[1,16,2048]{2,1,0:T(8,128)(2,1)S(1)} %get-tuple-element.8), channel_id=1, source_target_pairs={{0,28},{2,30},{4,24},{6,26},{8,20},{10,22},{12,16},{14,18},{16,12}... | collective-permute-start | bytes 196616 | tf_op jit(solution)/shard_map/ppermute | solution.py:137
  499.3 13.7 %collective-permute-start.14 = (bf16[1,16,2048]{2,1,0:T(8,128)(2,1)S(1)}, bf16[1,16,2048]{2,1,0:T(8,128)(2,1)S(1)}, u32[]{:S(2)}, u32[]{:S(2)}) collective-permute-start(bf16[1,16,2048]{2,1,0:T(8,128)(2,1)S(1)} %get-tuple-element.7), channel_id=1, source_target_pairs={{0,30},{2,28},{4,26},{6,24},{8,22},{10,20},{12,18},{14,16},{16,14}... | collective-permute-start | bytes 196616 | tf_op jit(solution)/shard_map/ppermute | solution.py:137
  (3 other events, 169.2 us)
Sparse Core Ops, SparseCore 0:
  57.3 107.8 reduce-scatter.1
  166.7 21.0 all-gather.5
  189.9 50.2 all-gather.11
  242.2 49.0 all-gather.13
  293.3 72.7 all-gather.9
  368.1 73.1 all-gather.7
